TPU v7x, 256 devices: a whole 4x4x8 slice. The times are simulated.
256 devices in a mesh: rows: 32 (over y, z), tensor: 8 (over x, core).
Axes of the slice: x: 4, y: 4, z: 8, core: 2. Of those that a mesh axis runs over, the one named last changes fastest.
Arguments:
- token_ids: int32 [256, 4], replicated, may hold values from 0 to 65535
- cache_lengths: int32 [256], P('rows'), may hold values from 160 to 1280, as said below
- doc_ids: int32 [256], replicated, may hold values from 0 to 31
- embed_table: bfloat16 [65536, 8192], P('tensor', 'rows'), may hold values from -10.5 to 10.5
- cache_keys: bfloat16 [256, 1280, 1024], P('rows', None, 'tensor'), may hold values from -700 to 700
- cache_values: bfloat16 [256, 1280, 1024], P('rows', None, 'tensor'), may hold values from -6 to 6
- decode_gain: float32 [8192], P('rows'), may hold values from 0.1 to 1.9
- decode_query: bfloat16 [8192, 8192], P('rows', 'tensor'), may hold values from -0.0625 to 0.0625
- decode_key: bfloat16 [8192, 1024], P('rows', 'tensor'), may hold values from -0.0625 to 0.0625
- decode_value: bfloat16 [8192, 1024], P('rows', 'tensor'), may hold values from -0.0625 to 0.0625
- decode_out: bfloat16 [8192, 8192], P('tensor', 'rows'), may hold values from -0.0625 to 0.0625
- reduce_gain: float32 [8192], P('rows'), may hold values from 0.8 to 10
- reduce_query: bfloat16 [8192, 8192], P('rows', 'tensor'), may hold values from -0.0625 to 0.0625
- reduce_key: bfloat16 [8192, 1024], P('rows', 'tensor'), may hold values from -0.0625 to 0.0625
- reduce_value: bfloat16 [8192, 1024], P('rows', 'tensor'), may hold values from -0.0625 to 0.0625
- reduce_out: bfloat16 [8192, 8192], P('tensor', 'rows'), may hold values from -0.0625 to 0.0625
Outputs:
- reduced: bfloat16 [1024, 8192], P(None, 'rows')
Inputs may be any that keep to these rules, and one draw needn't show every extreme that they name: Passage row c holds cache entries at positions below cache_lengths[c]; one row in every draw has a full cache of 1280.
All inputs are finite; a program needn't handle non-finite values.
Results may differ from a plain program's by a relative error of at most 0.035.
The roundings to bfloat16 on the way count: a program that leaves them out, or rounds other values in their place, can miss the bound.
Values may be sent and summed in bfloat16 or wider, within the bound.
A program may use at most 64 MiB of HBM per device.

v0:
```python
import jax
import jax.numpy as jnp
from jax import lax
from jax.sharding import PartitionSpec as P

D = 8192
HEAD_DIM = 128
EPSILON = 1e-05
ROPE_BASE = 500000.0


def rotate(vectors, positions):
    half_dim = vectors.shape[-1] // 2
    frequencies = ROPE_BASE ** (-2.0 * jnp.arange(half_dim, dtype=jnp.float32) / vectors.shape[-1])
    angles = positions.astype(jnp.float32)[..., None] * frequencies
    cosine = jnp.cos(angles)
    sine_part = jnp.sin(angles)
    lower_half = vectors[..., :half_dim]
    upper_half = vectors[..., half_dim:]
    return jnp.concatenate(
        [
            lower_half * cosine - upper_half * sine_part,
            upper_half * cosine + lower_half * sine_part,
        ],
        axis=-1,
    )


def width_total(partial_value):
    return lax.psum(partial_value, "tensor")


def row_scale(squares):
    summed = lax.psum(squares, "rows")
    return lax.rsqrt(summed / D + EPSILON)


def head_terms(normed, matrices):
    return lax.psum_scatter(
        jnp.concatenate(
            [jnp.dot(normed, matrix, preferred_element_type=jnp.float32) for matrix in matrices],
            axis=1,
        ),
        "rows",
        scatter_dimension=0,
        tiled=True,
    )


def head_mix(attended, matrix):
    return jnp.dot(
        lax.all_gather(attended, "rows", axis=0, tiled=True),
        matrix,
        preferred_element_type=jnp.float32,
    )


def per_device(
    token_ids,
    cache_lengths,
    doc_ids,
    embed_table,
    cache_keys,
    cache_values,
    decode_gain,
    decode_query,
    decode_key,
    decode_value,
    decode_out,
    reduce_gain,
    reduce_query,
    reduce_key,
    reduce_value,
    reduce_out,
):
    step_count = token_ids.shape[1]
    passage_count = token_ids.shape[0]
    token_count = passage_count * step_count
    own_passages = cache_lengths.shape[0]
    own_tokens = own_passages * step_count
    row_first = lax.axis_index("rows") * own_tokens
    query_cols = decode_query.shape[1]
    kv_cols = decode_key.shape[1]
    local_heads = query_cols // HEAD_DIM
    local_kv = kv_cols // HEAD_DIM
    group_size = local_heads // local_kv
    score_scale = HEAD_DIM ** (-0.5)
    step_ids = jnp.arange(step_count, dtype=jnp.int32)
    vocab_part = embed_table.shape[0]
    local_ids = token_ids.reshape(token_count) - lax.axis_index("tensor") * vocab_part
    inside = (local_ids >= 0) & (local_ids < vocab_part)
    picked = jnp.take(embed_table, jnp.clip(local_ids, 0, vocab_part - 1), axis=0)
    picked = jnp.where(inside[:, None], picked.astype(jnp.float32), 0.0)
    embedded = width_total(picked)
    dec_scale = row_scale(jnp.sum(embedded * embedded, axis=1))
    normed = (embedded * decode_gain[None, :]).astype(jnp.bfloat16)
    projected = head_terms(normed, (decode_query, decode_key, decode_value))
    projected = projected * lax.dynamic_slice_in_dim(dec_scale, row_first, own_tokens, 0)[:, None]
    positions = (cache_lengths[:, None] + step_ids[None, :]).reshape(own_tokens, 1)
    queries = rotate(
        projected[:, :query_cols].reshape(own_tokens, local_heads, HEAD_DIM), positions
    ).astype(jnp.bfloat16)
    keys_new = rotate(
        projected[:, query_cols : query_cols + kv_cols].reshape(own_tokens, local_kv, HEAD_DIM),
        positions,
    ).astype(jnp.bfloat16)
    values_new = projected[:, query_cols + kv_cols :].astype(jnp.bfloat16)
    queries = queries.reshape(own_passages, step_count, local_kv, group_size, HEAD_DIM)
    keys_new = keys_new.reshape(own_passages, step_count, local_kv, HEAD_DIM)
    values_new = values_new.reshape(own_passages, step_count, local_kv, HEAD_DIM)
    capacity = cache_keys.shape[1]
    keys_old = cache_keys.reshape(own_passages, capacity, local_kv, HEAD_DIM)
    values_old = cache_values.reshape(own_passages, capacity, local_kv, HEAD_DIM)
    new_scores = (
        jnp.einsum("rskgd,rtkd->rskgt", queries, keys_new, preferred_element_type=jnp.float32)
        * score_scale
    )
    causal = step_ids[None, :] <= step_ids[:, None]
    new_scores = jnp.where(causal[None, :, None, None, :], new_scores, -jnp.inf)
    old_scores = (
        jnp.einsum("rskgd,rckd->rskgc", queries, keys_old, preferred_element_type=jnp.float32)
        * score_scale
    )
    slot_ids = jnp.arange(capacity, dtype=jnp.int32)
    live_mask = slot_ids[None, :] < cache_lengths[:, None]
    old_scores = jnp.where(live_mask[:, None, None, None, :], old_scores, -jnp.inf)
    highest = jnp.maximum(jnp.max(old_scores, axis=-1), jnp.max(new_scores, axis=-1))
    old_exp = jnp.exp(old_scores - highest[..., None])
    new_exp = jnp.exp(new_scores - highest[..., None])
    summed = jnp.sum(old_exp, axis=-1) + jnp.sum(new_exp, axis=-1)
    old_weights = (old_exp / summed[..., None]).astype(jnp.bfloat16)
    new_weights = (new_exp / summed[..., None]).astype(jnp.bfloat16)
    attended = jnp.einsum(
        "rskgc,rckd->rskgd", old_weights, values_old, preferred_element_type=jnp.float32
    )
    attended = attended + jnp.einsum(
        "rskgt,rtkd->rskgd", new_weights, values_new, preferred_element_type=jnp.float32
    )
    attended = attended.reshape(own_tokens, query_cols).astype(jnp.bfloat16)
    partial_value = head_mix(attended, decode_out)
    summary = (embedded + width_total(partial_value)).astype(jnp.bfloat16)
    summary_wide = summary.astype(jnp.float32)
    red_scale = row_scale(jnp.sum(summary_wide * summary_wide, axis=1))
    normed_red = (summary_wide * reduce_gain[None, :]).astype(jnp.bfloat16)
    passage_index = jnp.arange(passage_count, dtype=jnp.int32)
    earlier = jnp.sum(
        (
            (doc_ids[None, :] == doc_ids[:, None])
            & (passage_index[None, :] < passage_index[:, None])
        ).astype(jnp.int32),
        axis=1,
    )
    doc_positions = (earlier[:, None] * step_count + step_ids[None, :]).reshape(token_count, 1)
    doc_tokens = (doc_ids[:, None] + jnp.zeros_like(step_ids)[None, :]).reshape(token_count)
    own_positions = lax.dynamic_slice_in_dim(doc_positions, row_first, own_tokens, 0)
    own_scale = lax.dynamic_slice_in_dim(red_scale, row_first, own_tokens, 0)[:, None]
    projected = head_terms(normed_red, (reduce_query, reduce_key, reduce_value)) * own_scale
    queries_red = rotate(
        projected[:, :query_cols].reshape(own_tokens, local_heads, HEAD_DIM), own_positions
    ).astype(jnp.bfloat16)
    keys_own = (
        rotate(
            projected[:, query_cols : query_cols + kv_cols].reshape(own_tokens, local_kv, HEAD_DIM),
            own_positions,
        )
        .astype(jnp.bfloat16)
        .reshape(own_tokens, kv_cols)
    )
    values_own = projected[:, query_cols + kv_cols :].astype(jnp.bfloat16)
    keys_red, values_red = (
        lax.all_gather(keys_own, "rows", axis=0, tiled=True),
        lax.all_gather(values_own, "rows", axis=0, tiled=True),
    )
    queries_red = queries_red.reshape(own_tokens, local_kv, group_size, HEAD_DIM)
    keys_red = keys_red.reshape(token_count, local_kv, HEAD_DIM)
    values_red = values_red.reshape(token_count, local_kv, HEAD_DIM)
    token_index = jnp.arange(token_count, dtype=jnp.int32)
    own_index = row_first + jnp.arange(own_tokens, dtype=jnp.int32)
    own_docs = lax.dynamic_slice_in_dim(doc_tokens, row_first, own_tokens, 0)
    allowed = (own_docs[:, None] == doc_tokens[None, :]) & (
        token_index[None, :] <= own_index[:, None]
    )
    red_scores = (
        jnp.einsum("tkgd,ukd->tkgu", queries_red, keys_red, preferred_element_type=jnp.float32)
        * score_scale
    )
    red_scores = jnp.where(allowed[:, None, None, :], red_scores, -jnp.inf)
    red_high = jnp.max(red_scores, axis=-1)
    red_exp = jnp.exp(red_scores - red_high[..., None])
    red_weights = (red_exp / jnp.sum(red_exp, axis=-1)[..., None]).astype(jnp.bfloat16)
    red_out = jnp.einsum(
        "tkgu,ukd->tkgd", red_weights, values_red, preferred_element_type=jnp.float32
    )
    red_out = red_out.reshape(own_tokens, query_cols).astype(jnp.bfloat16)
    return (summary_wide + width_total(head_mix(red_out, reduce_out))).astype(jnp.bfloat16)


def solution(mesh):
    return jax.shard_map(
        per_device,
        mesh=mesh,
        in_specs=(
            P(),
            P("rows"),
            P(),
            P("tensor", "rows"),
            P("rows", None, "tensor"),
            P("rows", None, "tensor"),
            P("rows"),
            P("rows", "tensor"),
            P("rows", "tensor"),
            P("rows", "tensor"),
            P("tensor", "rows"),
            P("rows"),
            P("rows", "tensor"),
            P("rows", "tensor"),
            P("rows", "tensor"),
            P("tensor", "rows"),
        ),
        out_specs=P(None, "rows"),
        check_vma=False,
    )
```

profile of v0, /device:TPU:8, one launch (start us, length us, event | category | flops | bytes accessed | tf_op | source)
XLA Modules:
  0.0 966.4 jit_solution(12764112662389864731)
XLA Ops:
  6.5 0.8 subtract_clamp_fusion
  7.8 0.7 compare_and_fusion.1
  8.8 6.2 gather_fusion
  15.0 1.3 convert_select_fusion
  16.4 70.6 %all-reduce.4.cloned.1.call-done = f32[1024,256]{1,0:T(8,128)} async-done(((f32[1024,256]{1,0:T(8,128)}), f32[1024,256]{1,0:T(8,128)}) %all-reduce.4.cloned.1.call-update) | async-done | bytes 1048592 | tf_op jit(solution)/shard_map/psum | solution.py:30
  87.1 1.4 multiply_reduce_fusion
  88.6 0.8 fusion.72
  90.0 2.8 pad_maximum_fusion
  92.8 5.9 copy.69
  98.8 0.6 copy-done.7
  100.4 63.5 %psum.36 = f32[1024]{0:T(1024)S(1)} all-reduce(f32[1024]{0:T(1024)S(1)} %get-tuple-element.7), channel_id=1, replica_groups=mesh['rows'=32,'tensor'=8] {'rows'}, use_global_device_ids=true, to_apply=%region_3.4 | all-reduce | flops 1024 | bytes 8192 | tf_op jit(solution)/shard_map/psum | solution.py:34
  164.0 160.3 %reduce-scatter.7.cloned.1.call-done = f32[32,1280]{1,0:T(8,128)} async-done(((f32[1024,1280]{1,0:T(8,128)}), f32[32,1280]{1,0:T(8,128)}) %reduce-scatter.7.cloned.1.call-update) | async-done | bytes 163856 | tf_op jit(solution)/shard_map/reduce_scatter | solution.py:39
  324.2 1.0 broadcast_multiply_fusion.1
  325.6 1.1 fusion.69
  328.5 0.6 copy.86
  329.2 75.8 %all-gather.3.cloned.1.call-done = bf16[1024,1024]{1,0:T(8,128)(2,1)} async-done(((bf16[32,1024]{1,0:T(8,128)(2,1)}), bf16[1024,1024]{1,0:T(8,128)(2,1)}) %all-gather.3.cloned.1.call-update) | async-done | bytes 2097168 | tf_op jit(solution)/shard_map/all_gather | solution.py:52
  405.0 3.3 fusion.75
  408.3 66.2 %all-reduce.6.cloned.1.call-done = f32[1024,256]{1,0:T(8,128)} async-done(((f32[1024,256]{1,0:T(8,128)}), f32[1024,256]{1,0:T(8,128)}) %all-reduce.6.cloned.1.call-update) | async-done | bytes 1048592 | tf_op jit(solution)/shard_map/psum | solution.py:30
  474.6 1.8 fusion.22
  476.4 1.8 fusion.32
  478.9 2.8 pad_maximum_fusion.1
  481.6 5.9 copy.71
  488.0 63.5 %psum.38 = f32[1024]{0:T(1024)S(1)} all-reduce(f32[1024]{0:T(1024)S(1)} %get-tuple-element.5), channel_id=1, replica_groups=mesh['rows'=32,'tensor'=8] {'rows'}, use_global_device_ids=true, to_apply=%region_11.12 | all-reduce | flops 1024 | bytes 8192 | tf_op jit(solution)/shard_map/psum | solution.py:34
  551.7 161.6 %reduce-scatter.9.cloned.1.call-done = f32[32,1280]{1,0:T(8,128)} async-done(((f32[1024,1280]{1,0:T(8,128)}), f32[32,1280]{1,0:T(8,128)}) %reduce-scatter.9.cloned.1.call-update) | async-done | bytes 163856 | tf_op jit(solution)/shard_map/reduce_scatter | solution.py:39
  713.2 1.0 broadcast_multiply_fusion
  714.5 47.5 %all_gather.14 = bf16[1024,128]{1,0:T(8,128)(2,1)S(1)} all-gather(bf16[32,128]{1,0:T(8,128)(2,1)S(1)} %pad_maximum_fusion.5), channel_id=1, replica_groups=mesh['rows'=32,'tensor'=8] {'rows'}, dimensions={0}, use_global_device_ids=true | all-gather | bytes 270336 | tf_op jit(solution)/shard_map/all_gather | solution.py:171
  762.1 47.8 %all_gather.13 = bf16[1024,128]{1,0:T(8,128)(2,1)S(1)} all-gather(bf16[32,128]{1,0:T(8,128)(2,1)S(1)} %slice.100), channel_id=1, replica_groups=mesh['rows'=32,'tensor'=8] {'rows'}, dimensions={0}, use_global_device_ids=true | all-gather | bytes 270336 | tf_op jit(solution)/shard_map/all_gather | solution.py:172
  811.2 0.6 copy.85
  811.9 75.9 %all-gather.5.cloned.1.call-done = bf16[1024,1024]{1,0:T(8,128)(2,1)} async-done(((bf16[32,1024]{1,0:T(8,128)(2,1)}), bf16[1024,1024]{1,0:T(8,128)(2,1)}) %all-gather.5.cloned.1.call-update) | async-done | bytes 2097168 | tf_op jit(solution)/shard_map/all_gather | solution.py:52
  887.7 3.4 fusion.76
  891.1 66.3 %all-reduce.8.cloned.1.call-done = f32[1024,256]{1,0:T(8,128)} async-done(((f32[1024,256]{1,0:T(8,128)}), f32[1024,256]{1,0:T(8,128)}) %all-reduce.8.cloned.1.call-update) | async-done | bytes 1048592 | tf_op jit(solution)/shard_map/psum | solution.py:30
  957.4 2.1 fusion.23
  (94 shorter events, 7.5 us)
Async XLA Ops:
  6.5 319.0 %copy-start = (bf16[8,1280,128]{2,1,0:T(8,128)(2,1)S(1)}, bf16[8,1280,128]{2,1,0:T(8,128)(2,1)}, u32[]{:S(2)}) copy-start(bf16[8,1280,128]{2,1,0:T(8,128)(2,1)} %param.20) | copy-start | bytes 7864324
  6.5 80.5 %all-reduce.4.cloned.1.call-start = ((), (), s32[]{:S(2)}) async-start(), calls=%async_computation.2 | async-start | bytes 2097152 | tf_op jit(solution)/shard_map/psum | solution.py:30
  8.8 78.3 %copy-start.9 = (f32[256]{0:T(256)S(1)}, f32[256]{0:T(256)}, u32[]{:S(2)}) copy-start(f32[256]{0:T(256)} %param.22) | copy-start | bytes 3076
  16.4 72.2 %copy-start.1 = (bf16[256,1024]{1,0:T(8,128)(2,1)S(1)}, bf16[256,1024]{1,0:T(8,128)(2,1)}, u32[]{:S(2)}) copy-start(bf16[256,1024]{1,0:T(8,128)(2,1)} %param.23) | copy-start | bytes 1572868
  16.4 307.8 %reduce-scatter.7.cloned.1.call-start = ((), (), s32[]{:S(2)}) async-start(), calls=%async_computation.7 | async-start | bytes 5406720 | tf_op jit(solution)/shard_map/reduce_scatter | solution.py:39
  88.5 0.8 copy-start.2
  88.5 1.1 copy-start.3
  98.7 0.7 copy-start.7
  98.7 1.1 copy-start.8
  98.8 306.2 %all-gather.3.cloned.1.call-start = ((), (), s32[]{:S(2)}) async-start(), calls=%async_computation.3 | async-start | bytes 2162688 | tf_op jit(solution)/shard_map/all_gather | solution.py:52
  325.6 2.3 copy-start.10
  327.9 77.1 %copy-start.11 = (bf16[1024,256]{1,0:T(8,128)(2,1)S(1)}, bf16[1024,256]{1,0:T(8,128)(2,1)}, u32[]{:S(2)}) copy-start(bf16[1024,256]{1,0:T(8,128)(2,1)} %param.26) | copy-start | bytes 1572868
  329.1 145.4 %all-reduce.6.cloned.1.call-start = ((), (), s32[]{:S(2)}) async-start(), calls=%async_computation.4 | async-start | bytes 2097152 | tf_op jit(solution)/shard_map/psum | solution.py:30
  408.3 68.1 %copy-start.6 = (f32[256]{0:T(256)S(1)}, f32[256]{0:T(256)}, u32[]{:S(2)}) copy-start(f32[256]{0:T(256)} %param.27) | copy-start | bytes 3076
  408.3 305.0 %reduce-scatter.9.cloned.1.call-start = ((), (), s32[]{:S(2)}) async-start(), calls=%async_computation.8 | async-start | bytes 5406720 | tf_op jit(solution)/shard_map/reduce_scatter | solution.py:39
  476.3 1.9 copy-start.4
  476.3 2.2 copy-start.5
  487.6 400.1 %all-gather.5.cloned.1.call-start = ((), (), s32[]{:S(2)}) async-start(), calls=%async_computation.5 | async-start | bytes 2162688 | tf_op jit(solution)/shard_map/all_gather | solution.py:52
  811.8 145.6 %all-reduce.8.cloned.1.call-start = ((), (), s32[]{:S(2)}) async-start(), calls=%async_computation.6 | async-start | bytes 2097152 | tf_op jit(solution)/shard_map/psum | solution.py:30
Sparse Core Ops, SparseCore 0:
  16.5 70.5 all-reduce.3
  98.9 225.3 reduce-scatter.6
  329.3 75.6 all-gather.2
  408.4 66.1 all-reduce.5
  487.7 225.4 reduce-scatter.8
  811.9 75.7 all-gather.4
  891.3 66.1 all-reduce.7
where the time goes:
time: 967 us; the launch traced here: 966 us
  waiting for transfers between devices  677 us (70%)
  blocking collectives  222 us (23%)
  local copies, waits for them, and re-layouts  21.6 us (2%)
  other arithmetic  17.9 us (2%)
  between operations  13.9 us (1%)
  matrix products  13.7 us (1%)
    reduce_scatter x2, waiting for transfers between devices, head_terms(): lax.psum_scatter(jnp.concatenate([jnp.dot(normed, matrix, preferred_eleme...  322 us
    psum x3, waiting for transfers between devices, width_total(): return lax.psum(partial_value, 'tensor')  203 us
    all_gather x2, waiting for transfers between devices, head_mix(): lax.all_gather(attended, 'rows', axis=0, tiled=True)  152 us
    psum x2, blocking collectives, row_scale(): summed = lax.psum(squares, 'rows')  127 us
    all_gather x1, blocking collectives, per_device(): lax.all_gather(values_own, 'rows', axis=0, tiled=True)  47.8 us
    all_gather x1, blocking collectives, per_device(): lax.all_gather(keys_own, 'rows', axis=0, tiled=True)  47.5 us
  transfers between devices with their start and end apart: 7, of which 7 were waited for; matrix products, arithmetic and copies ran while one was open for 0% of the time, Pallas kernels for 0%

commit v1 on v0

--- a/solution.py
+++ b/solution.py
@@ -7,6 +7,9 @@
 HEAD_DIM = 128
 EPSILON = 1e-05
 ROPE_BASE = 500000.0
+play_terms = lambda inner_x: jnp.concatenate(
+    lax.all_to_all(jnp.stack([inner_x] * lax.axis_size("rows")), "rows", 0, 0), axis=0
+)
 
 
 def rotate(vectors, positions):
@@ -48,11 +51,7 @@
 
 
 def head_mix(attended, matrix):
-    return jnp.dot(
-        lax.all_gather(attended, "rows", axis=0, tiled=True),
-        matrix,
-        preferred_element_type=jnp.float32,
-    )
+    return jnp.dot(play_terms(attended), matrix, preferred_element_type=jnp.float32)
 
 
 def per_device(

time: 967 us -> 902 us (0.933)
  waiting for transfers between devices: 677 us -> 525 us
  blocking collectives: 222 us -> 313 us
    all_gather x2 -> x0, waiting for transfers between devices: 152 us -> none  [head_mix(): lax.all_gather(attended, 'rows', axis=0, tiled=True)]
    all_to_all x0 -> x2, blocking collectives: none -> 86.3 us  [lax.all_to_all(jnp.stack([inner_x] * lax.axis_size('rows')), 'rows', 0, 0)]
  transfers between devices with their start and end apart: 7 -> 5, of which waited for: 7 -> 5; matrix products, arithmetic and copies ran while one was open for 0% -> 0% of each run, Pallas kernels for 0% -> 0%
where the time goes in v1:
time: 902 us; the launch traced here: 901 us
  waiting for transfers between devices  525 us (58%)
  blocking collectives  313 us (35%)
  local copies, waits for them, and re-layouts  20.8 us (2%)
  other arithmetic  17.9 us (2%)
  between operations  13.6 us (2%)
  matrix products  10.5 us (1%)
    reduce_scatter x2, waiting for transfers between devices, head_terms(): lax.psum_scatter(jnp.concatenate([jnp.dot(normed, matrix, preferred_eleme...  321 us
    psum x3, waiting for transfers between devices, width_total(): return lax.psum(partial_value, 'tensor')  203 us
    psum x2, blocking collectives, row_scale(): summed = lax.psum(squares, 'rows')  127 us
    all_to_all x2, blocking collectives, lax.all_to_all(jnp.stack([inner_x] * lax.axis_size('rows')), 'rows', 0, 0)  86.3 us
    all_gather x1, blocking collectives, per_device(): lax.all_gather(values_own, 'rows', axis=0, tiled=True)  52 us
    all_gather x1, blocking collectives, per_device(): lax.all_gather(keys_own, 'rows', axis=0, tiled=True)  47.6 us
  transfers between devices with their start and end apart: 5, of which 5 were waited for; matrix products, arithmetic and copies ran while one was open for 0% of the time, Pallas kernels for 0%

profile of v1, /device:TPU:8, one launch (start us, length us, event | category | flops | bytes accessed | tf_op | source)
XLA Modules:
  0.0 901.1 jit_solution(7796679217592552730)
XLA Ops:
  6.5 0.8 subtract_clamp_fusion
  7.8 0.7 compare_and_fusion.1
  8.8 6.2 gather_fusion
  15.0 1.3 convert_select_fusion
  16.4 70.6 %all-reduce.4.cloned.1.call-done = f32[1024,256]{1,0:T(8,128)} async-done(((f32[1024,256]{1,0:T(8,128)}), f32[1024,256]{1,0:T(8,128)}) %all-reduce.4.cloned.1.call-update) | async-done | bytes 1048592 | tf_op jit(solution)/shard_map/psum | solution.py:33
  87.1 1.4 multiply_reduce_fusion
  88.6 0.8 fusion.72
  90.0 2.8 pad_maximum_fusion
  92.8 5.9 copy.69
  98.8 0.6 copy-done.7
  100.4 63.7 %psum.36 = f32[1024]{0:T(1024)S(1)} all-reduce(f32[1024]{0:T(1024)S(1)} %get-tuple-element.7), channel_id=1, replica_groups=mesh['rows'=32,'tensor'=8] {'rows'}, use_global_device_ids=true, to_apply=%region_3.4 | all-reduce | flops 1024 | bytes 8192 | tf_op jit(solution)/shard_map/psum | solution.py:37
  164.2 160.2 %reduce-scatter.7.cloned.1.call-done = f32[32,1280]{1,0:T(8,128)} async-done(((f32[1024,1280]{1,0:T(8,128)}), f32[32,1280]{1,0:T(8,128)}) %reduce-scatter.7.cloned.1.call-update) | async-done | bytes 163856 | tf_op jit(solution)/shard_map/reduce_scatter | solution.py:42
  324.4 1.0 broadcast_multiply_fusion.1
  325.7 1.1 fusion.69
  326.8 0.5 fusion.70
  328.0 0.6 fusion.15
  328.9 51.5 %all_to_all.10 = bf16[32,32,1024]{2,1,0:T(8,128)(2,1)S(1)} all-to-all(bf16[32,32,1024]{2,1,0:T(8,128)(2,1)S(1)} %stack.4), channel_id=1, replica_groups=mesh['rows'=32,'tensor'=8] {'rows'}, dimensions={0} | all-to-all | bytes 4194304 | tf_op jit(solution)/shard_map/all_to_all | solution.py:11
  380.4 1.7 fusion.75
  382.2 66.6 %all-reduce.6.cloned.1.call-done = f32[1024,256]{1,0:T(8,128)} async-done(((f32[1024,256]{1,0:T(8,128)}), f32[1024,256]{1,0:T(8,128)}) %all-reduce.6.cloned.1.call-update) | async-done | bytes 1048592 | tf_op jit(solution)/shard_map/psum | solution.py:33
  448.8 1.8 fusion.22
  450.6 1.8 fusion.32
  453.1 2.8 pad_maximum_fusion.1
  455.9 5.9 copy.71
  462.3 63.7 %psum.38 = f32[1024]{0:T(1024)S(1)} all-reduce(f32[1024]{0:T(1024)S(1)} %get-tuple-element.5), channel_id=1, replica_groups=mesh['rows'=32,'tensor'=8] {'rows'}, use_global_device_ids=true, to_apply=%region_11.12 | all-reduce | flops 1024 | bytes 8192 | tf_op jit(solution)/shard_map/psum | solution.py:37
  526.1 161.2 %reduce-scatter.9.cloned.1.call-done = f32[32,1280]{1,0:T(8,128)} async-done(((f32[1024,1280]{1,0:T(8,128)}), f32[32,1280]{1,0:T(8,128)}) %reduce-scatter.9.cloned.1.call-update) | async-done | bytes 163856 | tf_op jit(solution)/shard_map/reduce_scatter | solution.py:42
  687.3 1.0 broadcast_multiply_fusion
  688.6 47.6 %all_gather.7 = bf16[1024,128]{1,0:T(8,128)(2,1)S(1)} all-gather(bf16[32,128]{1,0:T(8,128)(2,1)S(1)} %pad_maximum_fusion.5), channel_id=1, replica_groups=mesh['rows'=32,'tensor'=8] {'rows'}, dimensions={0}, use_global_device_ids=true | all-gather | bytes 270336 | tf_op jit(solution)/shard_map/all_gather | solution.py:170
  736.4 52.0 %all_gather.6 = bf16[1024,128]{1,0:T(8,128)(2,1)S(1)} all-gather(bf16[32,128]{1,0:T(8,128)(2,1)S(1)} %slice.100), channel_id=1, replica_groups=mesh['rows'=32,'tensor'=8] {'rows'}, dimensions={0}, use_global_device_ids=true | all-gather | bytes 270336 | tf_op jit(solution)/shard_map/all_gather | solution.py:171
  789.9 34.8 %all_to_all.11 = bf16[32,32,1024]{2,1,0:T(8,128)(2,1)S(1)} all-to-all(bf16[32,32,1024]{2,1,0:T(8,128)(2,1)S(1)} %stack.5), channel_id=1, replica_groups=mesh['rows'=32,'tensor'=8] {'rows'}, dimensions={0} | all-to-all | bytes 4194304 | tf_op jit(solution)/shard_map/all_to_all | solution.py:11
  824.6 1.7 fusion.76
  826.4 66.1 %all-reduce.8.cloned.1.call-done = f32[1024,256]{1,0:T(8,128)} async-done(((f32[1024,256]{1,0:T(8,128)}), f32[1024,256]{1,0:T(8,128)}) %all-reduce.8.cloned.1.call-update) | async-done | bytes 1048592 | tf_op jit(solution)/shard_map/psum | solution.py:33
  892.5 2.1 fusion.23
  (94 shorter events, 6.8 us)
Async XLA Ops:
  6.5 319.2 %copy-start = (bf16[8,1280,128]{2,1,0:T(8,128)(2,1)S(1)}, bf16[8,1280,128]{2,1,0:T(8,128)(2,1)}, u32[]{:S(2)}) copy-start(bf16[8,1280,128]{2,1,0:T(8,128)(2,1)} %param.20) | copy-start | bytes 7864324
  6.5 80.5 %all-reduce.4.cloned.1.call-start = ((), (), s32[]{:S(2)}) async-start(), calls=%async_computation.4 | async-start | bytes 2097152 | tf_op jit(solution)/shard_map/psum | solution.py:33
  8.8 78.3 %copy-start.9 = (f32[256]{0:T(256)S(1)}, f32[256]{0:T(256)}, u32[]{:S(2)}) copy-start(f32[256]{0:T(256)} %param.22) | copy-start | bytes 3076
  16.4 72.2 %copy-start.1 = (bf16[256,1024]{1,0:T(8,128)(2,1)S(1)}, bf16[256,1024]{1,0:T(8,128)(2,1)}, u32[]{:S(2)}) copy-start(bf16[256,1024]{1,0:T(8,128)(2,1)} %param.23) | copy-start | bytes 1572868
  16.4 308.0 %reduce-scatter.7.cloned.1.call-start = ((), (), s32[]{:S(2)}) async-start(), calls=%async_computation.7 | async-start | bytes 5406720 | tf_op jit(solution)/shard_map/reduce_scatter | solution.py:42
  88.5 0.8 copy-start.2
  88.5 1.1 copy-start.3
  98.7 0.7 copy-start.7
  98.7 1.1 copy-start.8
  98.8 350.1 %all-reduce.6.cloned.1.call-start = ((), (), s32[]{:S(2)}) async-start(), calls=%async_computation.5 | async-start | bytes 2097152 | tf_op jit(solution)/shard_map/psum | solution.py:33
  325.7 2.3 copy-start.10
  328.9 51.6 %copy-start.11 = (bf16[1024,256]{1,0:T(8,128)(2,1)S(1)}, bf16[1024,256]{1,0:T(8,128)(2,1)}, u32[]{:S(2)}) copy-start(bf16[1024,256]{1,0:T(8,128)(2,1)} %param.26) | copy-start | bytes 1572868
  382.2 68.4 %copy-start.6 = (f32[256]{0:T(256)S(1)}, f32[256]{0:T(256)}, u32[]{:S(2)}) copy-start(f32[256]{0:T(256)} %param.27) | copy-start | bytes 3076
  382.2 305.2 %reduce-scatter.9.cloned.1.call-start = ((), (), s32[]{:S(2)}) async-start(), calls=%async_computation.8 | async-start | bytes 5406720 | tf_op jit(solution)/shard_map/reduce_scatter | solution.py:42
  450.6 1.9 copy-start.4
  450.6 2.2 copy-start.5
  461.9 430.6 %all-reduce.8.cloned.1.call-start = ((), (), s32[]{:S(2)}) async-start(), calls=%async_computation.6 | async-start | bytes 2097152 | tf_op jit(solution)/shard_map/psum | solution.py:33
  789.9 34.8 %copy-start.12 = (bf16[1024,256]{1,0:T(8,128)(2,1)S(1)}, bf16[1024,256]{1,0:T(8,128)(2,1)}, u32[]{:S(2)}) copy-start(bf16[1024,256]{1,0:T(8,128)(2,1)} %param.31) | copy-start | bytes 1572868
Sparse Core Ops, SparseCore 0:
  16.5 70.5 all-reduce.3
  98.9 225.4 reduce-scatter.6
  382.3 66.4 all-reduce.5
  462.0 225.3 reduce-scatter.8
  826.5 65.9 all-reduce.7
